TPU v7x, 128 devices: a whole 4x4x4 slice. The times are simulated.
128 devices in a mesh: gy: 32 (over z, y, core), var: 4 (over x).
Axes of the slice: x: 4, y: 4, z: 4, core: 2. Of those that a mesh axis runs over, the one named last changes fastest.
Arguments:
- field: float32 [32, 32, 1024, 128], P('var', None, 'gy')
- factor_x: float32 [32, 16], replicated, may hold values from -1 to 1
- factor_y: float32 [1024, 64], P('gy'), may hold values from -0.1875 to 0.1875
- factor_z: float32 [128, 64], replicated, may hold values from -0.5 to 0.5
- factor_v: float32 [32, 16], replicated, may hold values from -1 to 1
Outputs:
- proj_z: float32 [128, 128], replicated
- proj_v: float32 [32, 32], replicated
- core_rms: float32 [], replicated
All inputs are finite; a program needn't handle non-finite values.
Results may differ from a plain program's by a relative error of at most 0.0003.
Values sent between devices are 32-bit elements; how exact they have to be, the bound alone decides.
No kernel may reach another device: no remote copies, remote signals or barrier semaphores. Data moves between devices by JAX's collectives and lax.ppermute only.
A program may use at most 192 MiB of HBM per device.

v0:
```python
import jax
import jax.numpy as jnp
from jax import lax
from jax.sharding import PartitionSpec as P

precise = lax.Precision.HIGHEST


def orth(mat):
    gram = jnp.dot(mat.T, mat, precision=precise)
    lower = jnp.linalg.cholesky(gram)
    return jax.scipy.linalg.solve_triangular(lower, mat.T, lower=True).T


def total_core(local_part):
    return lax.psum(local_part, ("gy", "var"))


def per_device(field, factor_x, factor_y, factor_z, factor_v):
    var_rows = field.shape[0]
    var_start = lax.axis_index("var") * var_rows
    local_v = lax.dynamic_slice_in_dim(factor_v, var_start, var_rows, 0)
    along_x = jnp.einsum("vxyz,xa->vayz", field, factor_x, precision=precise)
    partial_value = jnp.einsum("vayz,yb->vabz", along_x, factor_y, precision=precise)
    wide_z = jnp.einsum("vabz,vc->cabz", partial_value, local_v, precision=precise)
    fibres = lax.psum_scatter(wide_z, ("gy", "var"), scatter_dimension=3, tiled=True)
    z_count = fibres.shape[3]
    z_start = lax.axis_index(("gy", "var")) * z_count
    local_z = lax.dynamic_slice_in_dim(factor_z, z_start, z_count, 0)
    small_core = total_core(jnp.einsum("cabz,zr->cabr", fibres, local_z, precision=precise))
    rows_z = jnp.einsum("cabz,cabr->zr", fibres, small_core, precision=precise)
    raw_z = lax.all_gather(rows_z, ("gy", "var"), axis=0, tiled=True)
    new_z = orth(raw_z)
    proj_z = jnp.dot(new_z, new_z.T, precision=precise)
    wide_v = jnp.einsum("vabz,zr->vabr", partial_value, new_z, precision=precise)
    flat_v = wide_v.reshape(var_rows, -1)
    summed_v = lax.psum(flat_v, "gy")
    every_v = lax.all_gather(summed_v, "var", axis=0, tiled=True)
    gram_v = jnp.dot(every_v, every_v.T, precision=precise)
    new_v = orth(jnp.dot(gram_v, factor_v, precision=precise))
    proj_v = jnp.dot(new_v, new_v.T, precision=precise)
    core = jnp.dot(new_v.T, every_v, precision=precise)
    core_rms = jnp.sqrt(jnp.mean(core * core))
    return (proj_z, proj_v, core_rms)


def solution(mesh):
    in_specs = (P("var", None, "gy", None), P(), P("gy", None), P(), P())
    out_specs = (P(), P(), P())
    return jax.shard_map(
        per_device, mesh=mesh, in_specs=in_specs, out_specs=out_specs, check_vma=False
    )
```

profile of v0, /device:TPU:1, one launch (start us, length us, event | category | flops | bytes accessed | tf_op | source)
XLA Modules:
  0.0 1346.6 jit_solution(12369558590492828368)
XLA Ops:
  7.2 6.9 fusion.5
  14.1 4.1 convolution_bitcast_fusion
  18.2 2.0 copy-done.1
  20.2 5.2 copy.21
  25.4 122.6 %fusion.25 = f32[16,131072]{0,1} fusion(f32[8,131072]{1,0:T(8,128)} %bitcast.65, f32[32,16]{0,1:T(8,128)S(1)} %copy-done.3, s32[]{:T(128)S(6)} %select_n.14), kind=kOutput, calls=%fused_computation.35 | convolution fusion | flops 201326592 | bytes 71305216
  148.0 42.6 %copy.22 = f32[16,16,64,128]{2,1,0,3:T(8,128)} copy(f32[16,16,64,128]{0,3,2,1:T(8,128)} %bitcast.7) | data formatting | bytes 16777216 | tf_op jit(solution)/shard_map/vabz,vc->cabz/dot_general | solution.py:25
  190.9 668.2 %reduce-scatter.2.cloned.1.call-done = f32[16,16,64,1]{2,1,0,3:T(8,128)} async-done(((f32[16,16,64,128]{2,1,0,3:T(8,128)}), f32[16,16,64,1]{2,1,0,3:T(8,128)}) %reduce-scatter.2.cloned.1.call-update) | async-done | bytes 65552 | tf_op jit(solution)/shard_map/reduce_scatter | solution.py:26
  859.1 5.5 broadcast_multiply_fusion
  864.7 165.4 %all-reduce.4.cloned.1.call-done = f32[16,16,64,64]{3,2,1,0:T(8,128)} async-done(((f32[16,16,64,64]{3,2,1,0:T(8,128)}), f32[16,16,64,64]{3,2,1,0:T(8,128)}) %all-reduce.4.cloned.1.call-update) | async-done | bytes 4194320 | tf_op jit(solution)/shard_map/psum | solution.py:16
  1030.1 6.6 fusion.9
  1037.0 64.0 %all-reduce = f32[8192]{0:T(1024)S(1)} all-reduce(f32[8192]{0:T(1024)S(1)} %dynamic-update-slice.6), channel_id=2, replica_groups=mesh['gy'=32,'var'=4] {'gy','var'}, use_global_device_ids=true, to_apply=%add | all-reduce | flops 8192 | bytes 65536
  1101.5 5.8 cholesky.29
  1108.0 0.7 fusion.13
  1108.7 4.9 custom-call.14
  1113.9 6.6 fusion.14
  1120.5 4.7 reshape.38
  1125.3 104.6 %all-reduce.6.cloned.1.call-done = f32[8,65536]{1,0:T(8,128)} async-done(((f32[8,65536]{1,0:T(8,128)}), f32[8,65536]{1,0:T(8,128)}) %all-reduce.6.cloned.1.call-update) | async-done | bytes 2097168 | tf_op jit(solution)/shard_map/psum | solution.py:37
  1229.9 0.9 fusion.29
  1230.8 83.4 %all-gather.3.cloned.1.call-done = f32[32,65536]{1,0:T(8,128)} async-done(((f32[8,65536]{1,0:T(8,128)}), f32[32,65536]{1,0:T(8,128)}) %all-gather.3.cloned.1.call-update) | async-done | bytes 8388624 | tf_op jit(solution)/shard_map/all_gather | solution.py:38
  1314.2 10.7 fusion.30
  1325.2 1.5 cholesky.61
  1328.0 1.2 custom-call.15
  1329.5 0.8 fusion.33
  1330.3 7.5 fusion.8
  (35 shorter events, 4.0 us)
Async XLA Ops:
  7.2 183.6 %copy-start = (f32[128,64]{0,1:T(8,128)S(1)}, f32[128,64]{0,1:T(8,128)}, u32[]{:S(2)}) copy-start(f32[128,64]{0,1:T(8,128)} %param.8) | copy-start | bytes 98308
  7.2 6.9 copy-start.4
  7.2 851.9 %reduce-scatter.2.cloned.1.call-start = ((), (), s32[]{:S(2)}) async-start(), calls=%async_computation.1 | async-start | bytes 16908288 | tf_op jit(solution)/shard_map/reduce_scatter | solution.py:26
  18.2 2.0 copy-start.1
  20.2 5.3 copy-start.3
  190.7 839.4 %all-reduce.4.cloned.1.call-start = ((), (), s32[]{:S(2)}) async-start(), calls=%async_computation.2 | async-start | bytes 16777216 | tf_op jit(solution)/shard_map/psum | solution.py:16
  864.6 165.5 %copy-start.2 = (f32[16,16,64,1]{2,1,0,3:T(8,128)S(1)}, f32[16,16,64,1]{2,1,0,3:T(8,128)}, u32[]{:S(2)}) copy-start(f32[16,16,64,1]{2,1,0,3:T(8,128)} %reduce-scatter.2.cloned.1.call-done) | copy-start | bytes 196612
  864.6 365.3 %all-reduce.6.cloned.1.call-start = ((), (), s32[]{:S(2)}) async-start(), calls=%async_computation.3 | async-start | bytes 4194304 | tf_op jit(solution)/shard_map/psum | solution.py:37
  1125.2 189.0 %all-gather.3.cloned.1.call-start = ((), (), s32[]{:S(2)}) async-start(), calls=%async_computation.4 | async-start | bytes 10485760 | tf_op jit(solution)/shard_map/all_gather | solution.py:38
Sparse Core Ops, SparseCore 0:
  190.8 668.2 reduce-scatter.1
  864.7 165.3 all-reduce.3
  1125.3 104.5 all-reduce.5
  1231.5 82.6 all-gather.2
where the time goes:
time: 1350 us
  waiting for transfers between devices  1020 us (76%)
  matrix products  168 us (12%)
  blocking collectives  64 us (5%)
  local copies, waits for them, and re-layouts  55.3 us (4%)
  other arithmetic  21.6 us (2%)
  between operations  16.2 us (1%)
    reduce_scatter x1, waiting for transfers between devices, per_device(): lax.psum_scatter(wide_z, ('gy', 'var'), scatter_dimension=3, tiled=True)  668 us
    psum x1, waiting for transfers between devices, total_core(): return lax.psum(local_part, ('gy', 'var'))  165 us
    unnamed x1, matrix products  123 us
    psum x1, waiting for transfers between devices, per_device(): summed_v = lax.psum(flat_v, 'gy')  105 us
    all_gather x1, waiting for transfers between devices, per_device(): every_v = lax.all_gather(summed_v, 'var', axis=0, tiled=True)  83.4 us
    unnamed x1, blocking collectives  64 us
    dot_general x1, local copies, waits for them, and re-layouts, per_device(): jnp.einsum('vabz,vc->cabz', partial_value, local_v, precision=precise)  42.6 us
  transfers between devices with their start and end apart: 4, of which 4 were waited for; matrix products, arithmetic and copies ran while one was open for 0% of the time, Pallas kernels for 0%

commit v1 on v0

--- a/solution.py
+++ b/solution.py
@@ -4,6 +4,14 @@
 from jax.sharding import PartitionSpec as P
 
 precise = lax.Precision.HIGHEST
+
+
+def doubling_sum(block, name):
+    count, total = (lax.axis_size(name), block)
+    for far in [1 << k for k in range(count.bit_length() - 1)]:
+        swap = [(i, i ^ far) for i in range(count)]
+        total = total + lax.ppermute(total, name, swap)
+    return total
 
 
 def orth(mat):
@@ -34,7 +42,7 @@
     proj_z = jnp.dot(new_z, new_z.T, precision=precise)
     wide_v = jnp.einsum("vabz,zr->vabr", partial_value, new_z, precision=precise)
     flat_v = wide_v.reshape(var_rows, -1)
-    summed_v = lax.psum(flat_v, "gy")
+    summed_v = doubling_sum(flat_v, "gy")
     every_v = lax.all_gather(summed_v, "var", axis=0, tiled=True)
     gram_v = jnp.dot(every_v, every_v.T, precision=precise)
     new_v = orth(jnp.dot(gram_v, factor_v, precision=precise))

time: 1350 us -> 1430 us (1.059)
  waiting for transfers between devices: 1020 us -> 1100 us
    ppermute x0 -> x5, waiting for transfers between devices: none -> 183 us  [doubling_sum(): total = total + lax.ppermute(total, name, swap)]
    psum x1 -> x0, waiting for transfers between devices: 105 us -> none  [per_device(): summed_v = lax.psum(flat_v, 'gy')]
  transfers between devices with their start and end apart: 4 -> 8, of which waited for: 4 -> 8; matrix products, arithmetic and copies ran while one was open for 0% -> 0% of each run, Pallas kernels for 0% -> 0%
where the time goes in v1:
time: 1430 us; the launch traced here: 1420 us
  waiting for transfers between devices  1100 us (77%)
  matrix products  156 us (11%)
  blocking collectives  64.1 us (4%)
  local copies, waits for them, and re-layouts  54 us (4%)
  other arithmetic  24.1 us (2%)
  between operations  15.9 us (1%)
    reduce_scatter x1, waiting for transfers between devices, per_device(): lax.psum_scatter(wide_z, ('gy', 'var'), scatter_dimension=3, tiled=True)  667 us
    ppermute x5, waiting for transfers between devices, doubling_sum(): total = total + lax.ppermute(total, name, swap)  183 us
    psum x1, waiting for transfers between devices, total_core(): return lax.psum(local_part, ('gy', 'var'))  166 us
    unnamed x1, matrix products  111 us
    all_gather x1, waiting for transfers between devices, per_device(): every_v = lax.all_gather(summed_v, 'var', axis=0, tiled=True)  83.1 us
    unnamed x1, blocking collectives  64.1 us
    dot_general x1, local copies, waits for them, and re-layouts, per_device(): jnp.einsum('vabz,vc->cabz', partial_value, local_v, precision=precise)  42.7 us
  transfers between devices with their start and end apart: 8, of which 8 were waited for; matrix products, arithmetic and copies ran while one was open for 0% of the time, Pallas kernels for 0%

profile of v1, /device:TPU:1, one launch (start us, length us, event | category | flops | bytes accessed | tf_op | source)
XLA Modules:
  0.0 1419.7 jit_solution(8883208184153728233)
XLA Ops:
  7.2 6.9 fusion.5
  14.1 4.1 convolution_bitcast_fusion
  18.2 2.0 copy-done.1
  20.2 5.2 copy.21
  25.5 111.2 %fusion.25 = f32[16,131072]{0,1} fusion(f32[8,131072]{1,0:T(8,128)} %bitcast.65, f32[32,16]{0,1:T(8,128)S(1)} %copy-done.3, s32[]{:T(128)S(6)} %select_n.14), kind=kOutput, calls=%fused_computation.35 | convolution fusion | flops 201326592 | bytes 71305216
  136.6 42.7 %copy.22 = f32[16,16,64,128]{2,1,0,3:T(8,128)} copy(f32[16,16,64,128]{0,3,2,1:T(8,128)} %bitcast.7) | data formatting | bytes 16777216 | tf_op jit(solution)/shard_map/vabz,vc->cabz/dot_general | solution.py:33
  179.5 666.6 %reduce-scatter.2.cloned.1.call-done = f32[16,16,64,1]{2,1,0,3:T(8,128)} async-done(((f32[16,16,64,128]{2,1,0,3:T(8,128)}), f32[16,16,64,1]{2,1,0,3:T(8,128)}) %reduce-scatter.2.cloned.1.call-update) | async-done | bytes 65552 | tf_op jit(solution)/shard_map/reduce_scatter | solution.py:34
  846.2 5.5 broadcast_multiply_fusion
  851.7 165.8 %all-reduce.3.cloned.1.call-done = f32[16,16,64,64]{3,2,1,0:T(8,128)} async-done(((f32[16,16,64,64]{3,2,1,0:T(8,128)}), f32[16,16,64,64]{3,2,1,0:T(8,128)}) %all-reduce.3.cloned.1.call-update) | async-done | bytes 4194320 | tf_op jit(solution)/shard_map/psum | solution.py:24
  1017.6 6.6 fusion.9
  1024.5 64.1 %all-reduce = f32[8192]{0:T(1024)S(1)} all-reduce(f32[8192]{0:T(1024)S(1)} %dynamic-update-slice.6), channel_id=2, replica_groups=mesh['gy'=32,'var'=4] {'gy','var'}, use_global_device_ids=true, to_apply=%add | all-reduce | flops 8192 | bytes 65536
  1089.0 5.8 cholesky.29
  1096.2 4.9 custom-call.14
  1101.4 6.6 fusion.14
  1107.9 3.4 reshape.38
  1112.1 3.8 collective-permute-done
  1117.1 46.0 %collective-permute-done.1 = f32[8,65536]{1,0:T(8,128)S(1)} collective-permute-done((f32[8,65536]{1,0:T(8,128)S(1)}, f32[8,65536]{1,0:T(8,128)S(1)}, u32[]{:S(2)}, u32[]{:S(2)}) %collective-permute-start.1) | collective-permute-done | bytes 2097184 | tf_op jit(solution)/shard_map/ppermute | solution.py:13
  1165.1 45.6 %collective-permute-done.2 = f32[8,65536]{1,0:T(8,128)S(1)} collective-permute-done((f32[8,65536]{1,0:T(8,128)S(1)}, f32[8,65536]{1,0:T(8,128)S(1)}, u32[]{:S(2)}, u32[]{:S(2)}) %collective-permute-start.2) | collective-permute-done | bytes 2097184 | tf_op jit(solution)/shard_map/ppermute | solution.py:13
  1212.1 44.2 %collective-permute-done.3 = f32[8,65536]{1,0:T(8,128)S(1)} collective-permute-done((f32[8,65536]{1,0:T(8,128)S(1)}, f32[8,65536]{1,0:T(8,128)S(1)}, u32[]{:S(2)}, u32[]{:S(2)}) %collective-permute-start.3) | collective-permute-done | bytes 2097184 | tf_op jit(solution)/shard_map/ppermute | solution.py:13
  1256.5 2.0 collective-permute-start.4
  1258.5 43.7 %collective-permute-done.4 = f32[8,65536]{1,0:T(8,128)S(1)} collective-permute-done((f32[8,65536]{1,0:T(8,128)S(1)}, f32[8,65536]{1,0:T(8,128)S(1)}, u32[]{:S(2)}, u32[]{:S(2)}) %collective-permute-start.4) | collective-permute-done | bytes 2097184 | tf_op jit(solution)/shard_map/ppermute | solution.py:13
  1304.7 83.1 %all-gather.3.cloned.1.call-done = f32[32,65536]{1,0:T(8,128)} async-done(((f32[8,65536]{1,0:T(8,128)}), f32[32,65536]{1,0:T(8,128)}) %all-gather.3.cloned.1.call-update) | async-done | bytes 8388624 | tf_op jit(solution)/shard_map/all_gather | solution.py:46
  1387.8 10.4 fusion.30
  1403.6 7.5 fusion.8
  (47 shorter events, 16.1 us)
Async XLA Ops:
  7.2 172.2 %copy-start = (f32[128,64]{0,1:T(8,128)S(1)}, f32[128,64]{0,1:T(8,128)}, u32[]{:S(2)}) copy-start(f32[128,64]{0,1:T(8,128)} %param.8) | copy-start | bytes 98308
  7.2 6.9 copy-start.4
  7.2 839.0 %reduce-scatter.2.cloned.1.call-start = ((), (), s32[]{:S(2)}) async-start(), calls=%async_computation.1 | async-start | bytes 16908288 | tf_op jit(solution)/shard_map/reduce_scatter | solution.py:34
  18.2 2.0 copy-start.1
  20.2 5.3 copy-start.3
  179.3 838.3 %all-reduce.3.cloned.1.call-start = ((), (), s32[]{:S(2)}) async-start(), calls=%async_computation.2 | async-start | bytes 16777216 | tf_op jit(solution)/shard_map/psum | solution.py:24
  851.7 165.9 %copy-start.2 = (f32[16,16,64,1]{2,1,0,3:T(8,128)S(1)}, f32[16,16,64,1]{2,1,0,3:T(8,128)}, u32[]{:S(2)}) copy-start(f32[16,16,64,1]{2,1,0,3:T(8,128)} %reduce-scatter.2.cloned.1.call-done) | copy-start | bytes 196612
  851.7 536.1 %all-gather.3.cloned.1.call-start = ((), (), s32[]{:S(2)}) async-start(), calls=%async_computation.3 | async-start | bytes 10485760 | tf_op jit(solution)/shard_map/all_gather | solution.py:46
  1111.3 4.5 collective-permute-start
  1116.1 46.9 %collective-permute-start.1 = (f32[8,65536]{1,0:T(8,128)S(1)}, f32[8,65536]{1,0:T(8,128)S(1)}, u32[]{:S(2)}, u32[]{:S(2)}) collective-permute-start(f32[8,65536]{1,0:T(8,128)S(1)} %add.56), channel_id=1, source_target_pairs={{0,8},{4,12},{8,0},{12,4},{16,24},{20,28},{24,16},{28,20},{32,40},... | collective-permute-start | bytes 6291464 | tf_op jit(solution)/shard_map/ppermute | solution.py:13
  1163.3 47.5 %collective-permute-start.2 = (f32[8,65536]{1,0:T(8,128)S(1)}, f32[8,65536]{1,0:T(8,128)S(1)}, u32[]{:S(2)}, u32[]{:S(2)}) collective-permute-start(f32[8,65536]{1,0:T(8,128)S(1)} %add.57), channel_id=1, source_target_pairs={{0,16},{4,20},{8,24},{12,28},{16,0},{20,4},{24,8},{28,12},{32,48},... | collective-permute-start | bytes 6291464 | tf_op jit(solution)/shard_map/ppermute | solution.py:13
  1211.0 45.3 %collective-permute-start.3 = (f32[8,65536]{1,0:T(8,128)S(1)}, f32[8,65536]{1,0:T(8,128)S(1)}, u32[]{:S(2)}, u32[]{:S(2)}) collective-permute-start(f32[8,65536]{1,0:T(8,128)S(1)} %add.58), channel_id=1, source_target_pairs={{0,32},{4,36},{8,40},{12,44},{16,48},{20,52},{24,56},{28,60},{32,0... | collective-permute-start | bytes 6291464 | tf_op jit(solution)/shard_map/ppermute | solution.py:13
  1256.5 45.7 %collective-permute-start.4 = (f32[8,65536]{1,0:T(8,128)S(1)}, f32[8,65536]{1,0:T(8,128)S(1)}, u32[]{:S(2)}, u32[]{:S(2)}) collective-permute-start(f32[8,65536]{1,0:T(8,128)S(1)} %add.59), channel_id=1, source_target_pairs={{0,64},{4,68},{8,72},{12,76},{16,80},{20,84},{24,88},{28,92},{32,9... | collective-permute-start | bytes 6291464 | tf_op jit(solution)/shard_map/ppermute | solution.py:13
Sparse Core Ops, SparseCore 0:
  179.4 666.7 reduce-scatter.1
  851.8 165.7 all-reduce.2
  1303.9 83.8 all-gather.2
